TPU v7x, 128 devices: a whole 4x4x4 slice. The times are simulated.
128 devices in a mesh: region: 16 (over y, x_hi, core), ctx: 8 (over z, x_lo).
Axes of the slice: x: 4 (x_hi: 2, x_lo: 2; x = x_hi * 2 + x_lo), y: 4, z: 4, core: 2. Of those that a mesh axis runs over, the one named last changes fastest.
Arguments:
- tokens: bfloat16 [16, 4096, 1152], P('region', 'ctx'), may hold values from -6 to 6
- element_ids: int32 [16, 4096], P('region', 'ctx'), may hold values from 0 to 16383, as said below
- element_slot: int32 [16384], replicated, may hold values from 0 to 16383, as said below
- live_count: int32 [16, 8], P('region', 'ctx'), may hold values from 128 to 512
- cond_table: bfloat16 [16384, 1152], P(('region', 'ctx')), may hold values from -6 to 6
- w_ada: bfloat16 [1152, 3456], replicated, may hold values from -0.1875 to 0.1875
- b_ada: float32 [3456], replicated, may hold values from -3 to 3
- w_qkv: bfloat16 [1152, 3456], replicated, may hold values from -8 to 8
- w_out: bfloat16 [1152, 1152], replicated, may hold values from -0.1875 to 0.1875
Outputs:
- block_out: bfloat16 [16, 4096, 1152], P('region', 'ctx')
Inputs may be any that keep to these rules, and one draw needn't show every extreme that they name: element_ids: within each device's block of 512 patches (region r, positions c * 512 to (c + 1) * 512 - 1, device r * 8 + c of region+ctx), at most 6 patches name elements whose table row lies on one device (rows o * 128 to (o + 1) * 128 - 1); in every block some device is named by exactly 6 solid patches. element_slot is a permutation: element e is row element_slot[e] of cond_table.
All inputs are finite; a program needn't handle non-finite values.
Results may differ from a plain program's by a relative error of at most 0.027.
Values may be sent and summed in bfloat16 or wider, within the bound.
A program may use at most 192 MiB of HBM per device.

v0:
```python
import math
import jax
import jax.numpy as jnp
from jax import lax
from jax.sharding import PartitionSpec as P

HEADS = 16


def layer_modulate(device_tokens, mods, width):
    values = device_tokens.astype(jnp.float32)
    center = jnp.mean(values, axis=1, keepdims=True)
    spread = jnp.mean((values - center) ** 2, axis=1, keepdims=True)
    normed = (values - center) * lax.rsqrt(spread + 1e-06)
    shift = mods[:, :width]
    scale = mods[:, width : 2 * width]
    return (normed * (1.0 + scale) + shift).astype(jnp.bfloat16)


def per_device(
    tokens, element_ids, element_slot, live_count, cond_table, w_ada, b_ada, w_qkv, w_out
):
    device_tokens = tokens[0]
    tok_rows, width = device_tokens.shape
    owners = lax.axis_size(("region", "ctx"))
    elem_rows = cond_table.shape[0]
    capacity = max(2, 3 * tok_rows // (2 * owners))
    slots = element_slot[element_ids[0]]
    owner_index = slots // elem_rows
    local_row = slots % elem_rows
    position = jnp.arange(tok_rows, dtype=jnp.int32)
    solid = position < live_count[0, 0]
    earlier = (
        (owner_index[:, None] == owner_index[None, :])
        & (position[None, :] < position[:, None])
        & solid[None, :]
    )
    place_rank = jnp.sum(earlier.astype(jnp.int32), axis=1)
    target = jnp.where(solid, owner_index * capacity + place_rank, owners * capacity)
    requests = jnp.zeros((owners * capacity,), jnp.int32).at[target].set(local_row, mode="drop")
    asked = lax.all_to_all(
        requests.reshape(owners, capacity),
        ("region", "ctx"),
        split_axis=0,
        concat_axis=0,
        tiled=True,
    ).reshape(-1)
    pick_at = jnp.minimum(target, owners * capacity - 1)
    served = cond_table[asked].reshape(owners, capacity, width)
    replies = lax.all_to_all(served, ("region", "ctx"), split_axis=0, concat_axis=0, tiled=True)
    picked = replies.reshape(owners * capacity, width)[pick_at]
    activated = jnp.where(solid[:, None], jax.nn.silu(picked.astype(jnp.float32)), 0.0).astype(
        jnp.bfloat16
    )
    mods = (jnp.dot(activated, w_ada, preferred_element_type=jnp.float32) + b_ada).astype(
        jnp.bfloat16
    )
    mods = mods.astype(jnp.float32)
    modulated = layer_modulate(device_tokens, mods, width)
    qkv = jnp.dot(modulated, w_qkv, preferred_element_type=jnp.float32).astype(jnp.bfloat16)
    queries = qkv[:, :width]
    keys_here = qkv[:, width : 2 * width]
    values_here = qkv[:, 2 * width :]
    head_dim = width // HEADS
    inverse_root = 1.0 / math.sqrt(head_dim)
    query_heads = queries.reshape(tok_rows, HEADS, head_dim)
    initial = (
        jnp.full((HEADS, tok_rows), -1e30, jnp.float32),
        jnp.zeros((HEADS, tok_rows), jnp.float32),
        jnp.zeros((HEADS, tok_rows, head_dim), jnp.float32),
    )
    keys_piece = lax.all_gather(keys_here, "ctx", axis=0, tiled=True)
    values_piece = lax.all_gather(values_here, "ctx", axis=0, tiled=True)
    piece_rows = keys_piece.shape[0]
    block_rows = math.gcd(piece_rows, 512)
    key_blocks = keys_piece.reshape(piece_rows // block_rows, block_rows, HEADS, head_dim)
    value_blocks = values_piece.reshape(piece_rows // block_rows, block_rows, HEADS, head_dim)

    def advance(state, blocks):
        running_max, denominator, weighted = state
        key_block, value_block = blocks
        scores = (
            jnp.einsum("qhe,khe->hqk", query_heads, key_block, preferred_element_type=jnp.float32)
            * inverse_root
        )
        new_max = jnp.maximum(running_max, jnp.max(scores, axis=2))
        shrink = jnp.exp(running_max - new_max)
        expo = jnp.exp(scores - new_max[:, :, None])
        denominator = denominator * shrink + jnp.sum(expo, axis=2)
        weighted = weighted * shrink[:, :, None] + jnp.einsum(
            "hqk,khe->hqe",
            expo.astype(jnp.bfloat16),
            value_block,
            preferred_element_type=jnp.float32,
        )
        return ((new_max, denominator, weighted), None)

    result, _ = lax.scan(advance, initial, (key_blocks, value_blocks))
    final_max, denominator, weighted = result
    result = weighted / denominator[:, :, None]
    attended = jnp.transpose(result, (1, 0, 2)).reshape(tok_rows, width).astype(jnp.bfloat16)
    projected = jnp.dot(attended, w_out, preferred_element_type=jnp.float32)
    gate = mods[:, 2 * width :]
    output = (device_tokens.astype(jnp.float32) + gate * projected).astype(jnp.bfloat16)
    return output[None]


def solution(mesh):
    placed = (
        P("region", "ctx", None),
        P("region", "ctx"),
        P(),
        P("region", "ctx"),
        P(("region", "ctx"), None),
        P(),
        P(),
        P(),
        P(),
    )
    return jax.shard_map(
        per_device, mesh=mesh, in_specs=placed, out_specs=P("region", "ctx", None), check_vma=False
    )
```

profile of v0, /device:TPU:1, one launch (start us, length us, event | category | flops | bytes accessed | tf_op | source)
XLA Modules:
  0.0 791.2 jit_solution(2168846437949532841)
XLA Ops:
  14.5 21.0 %all_to_all.14 = s32[128,1,6]{2,1,0:T(1,128)S(1)} all-to-all(s32[128,1,6]{2,1,0:T(1,128)S(1)} %bitcast.77), channel_id=1, replica_groups=mesh['region'=16,'ctx'=8] {'region','ctx'}, dimensions={0} | all-to-all | bytes 6144 | tf_op jit(solution)/shard_map/all_to_all | solution.py:41
  53.4 29.6 %all-to-all-done.1 = bf16[128,6,1152]{2,1,0:T(8,128)(2,1)} async-done(((bf16[128,6,1152]{2,1,0:T(8,128)(2,1)}), bf16[128,6,1152]{2,1,0:T(8,128)(2,1)}, u32[]{:S(2)}, u32[]{:S(2)}) %all-to-all-start.1) | async-done | bytes 1769504 | tf_op jit(solution)/shard_map/all_to_all | solution.py:50
  100.3 11.4 %convolution_convert_fusion = bf16[512,3456]{1,0:T(8,128)(2,1)S(1)} fusion(bf16[1152,3456]{1,0:T(8,128)(2,1)} %param.18, bf16[1,512,1152]{2,1,0:T(8,128)(2,1)S(1)} %copy-done.2, f32[512,3456]{1,0:T(8,128)S(1)} %fusion.19, f32[512]{0:T(512)S(1)} %add_rsqrt_fusion, f32[512]{0:T(512)S(1)} %broadcast_multiply_fusion), kind=kOutput, calls=%fused_computation.28 | convolution fusion | flops 4082761728 | bytes 17403904 | tf_op jit(solution)/shard_map/dot_general | solution.py:60
  116.9 180.6 %all-gather.3.cloned.1.call-done = bf16[4096,1152]{1,0:T(8,128)(2,1)} async-done(((bf16[512,1152]{1,0:T(8,128)(2,1)}), bf16[4096,1152]{1,0:T(8,128)(2,1)}) %all-gather.3.cloned.1.call-update) | async-done | bytes 9437200 | tf_op jit(solution)/shard_map/all_gather | solution.py:72
  297.5 33.2 %reshape.260 = bf16[8,512,16,72]{3,2,1,0:T(8,128)(2,1)} reshape(bf16[4096,1152]{1,0:T(8,128)(2,1)} %all-gather.3.cloned.1.call-done) | data formatting | bytes 18874368 | tf_op jit(solution)/shard_map/reshape | solution.py:76
  330.7 21.5 %copy.32 = bf16[8,512,16,72]{1,3,2,0:T(8,128)(2,1)} copy(bf16[8,512,16,72]{3,2,1,0:T(8,128)(2,1)} %reshape.260) | data formatting | bytes 18874368
  352.2 136.0 %all-gather.5.cloned.1.call-done = bf16[4096,1152]{1,0:T(8,128)(2,1)} async-done(((bf16[512,1152]{1,0:T(8,128)(2,1)}), bf16[4096,1152]{1,0:T(8,128)(2,1)}) %all-gather.5.cloned.1.call-update) | async-done | bytes 9437200 | tf_op jit(solution)/shard_map/all_gather | solution.py:73
  488.2 33.2 %reshape.261 = bf16[8,512,16,72]{3,2,1,0:T(8,128)(2,1)} reshape(bf16[4096,1152]{1,0:T(8,128)(2,1)} %all-gather.5.cloned.1.call-done) | data formatting | bytes 18874368 | tf_op jit(solution)/shard_map/reshape | solution.py:77
  521.4 21.4 %copy.33 = bf16[8,512,16,72]{1,3,2,0:T(8,128)(2,1)} copy(bf16[8,512,16,72]{3,2,1,0:T(8,128)(2,1)} %reshape.261) | data formatting | bytes 18874368
  542.9 234.7 %while.15 = (s32[]{:T(128)}, f32[16,512]{1,0:T(8,128)S(1)}, f32[16,512]{1,0:T(8,128)S(1)}, f32[16,512,72]{1,2,0:T(8,128)}, bf16[8,512,16,72]{1,3,2,0:T(8,128)(2,...) while((s32[]{:T(128)}, f32[16,512]{1,0:T(8,128)S(1)}, ...), condition=%wide.region_7.8_spmd.clone, body=%wide.region_4.7_spmd.clone.sunk | while | flops 1243324416 | bytes 59114596 | solution.py:98
  542.9 9.7 %bitcast_reduce_fusion.2 = (f32[16,512]{1,0:T(8,128)S(1)}, f32[16,512,512]{2,1,0:T(8,128)}) fusion(bf16[512,16,72]{0,2,1:T(8,128)(2,1)} %get-tuple-element.196, bf16[8,512,16,72]{1,3,2,0:T(8,128)(2,1)} %get-tuple-element.195, s32[]{:T(128)} %get-tuple-element.182), kind=kOutput, calls=%fused_computation.5.clone.1 | convolution fusion | flops 612360192 | bytes 19169792 | tf_op jit(solution)/shard_map/while/body/eval_jaxpr/qhe,khe->hqk/dot_general | solution.py:83
  552.6 8.6 %fusion.67 = f32[16,512]{1,0:T(8,128)S(1)} fusion(f32[16,512,512]{2,1,0:T(8,128)} %get-tuple-element.170, f32[16,512]{1,0:T(8,128)S(1)} %select_maximum_fusion.2), kind=kLoop, calls=%fused_computation.8.clone.1 | loop fusion | flops 12574720 | bytes 16842752 | tf_op jit(solution)/shard_map/while/body/eval_jaxpr/reduce_sum | solution.py:89
  561.2 10.4 %fusion.69 = f32[16,512,72]{1,2,0:T(8,128)} fusion(f32[16,512,72]{1,2,0:T(8,128)} %get-tuple-element.185, f32[16,512,512]{2,1,0:T(8,128)} %get-tuple-element.170, f32[16,512]{1,0:T(8,128)S(1)} %select_maximum_fusion.2, bf16[8,512,16,72]{1,3,2,0:T(8,128)(2,1)} %get-tuple-element.197, s32[]{:T(128)} %get-tuple-element.182, ...), kind=kOutput, calls=%fused_computation.13.clone.1 | convolution fusion | flops 618332160 | bytes 22741504 | tf_op jit(solution)/shard_map/while/body/eval_jaxpr/hqk,khe->hqe/dot_general | solution.py:90
  571.6 9.7 %bitcast_reduce_fusion.2 = (f32[16,512]{1,0:T(8,128)S(1)}, f32[16,512,512]{2,1,0:T(8,128)}) fusion(bf16[512,16,72]{0,2,1:T(8,128)(2,1)} %get-tuple-element.196, bf16[8,512,16,72]{1,3,2,0:T(8,128)(2,1)} %get-tuple-element.195, s32[]{:T(128)} %get-tuple-element.182), kind=kOutput, calls=%fused_computation.5.clone.1 | convolution fusion | flops 612360192 | bytes 19169792 | tf_op jit(solution)/shard_map/while/body/eval_jaxpr/qhe,khe->hqk/dot_general | solution.py:83
  581.3 8.6 %fusion.67 = f32[16,512]{1,0:T(8,128)S(1)} fusion(f32[16,512,512]{2,1,0:T(8,128)} %get-tuple-element.170, f32[16,512]{1,0:T(8,128)S(1)} %select_maximum_fusion.2), kind=kLoop, calls=%fused_computation.8.clone.1 | loop fusion | flops 12574720 | bytes 16842752 | tf_op jit(solution)/shard_map/while/body/eval_jaxpr/reduce_sum | solution.py:89
  589.9 11.1 %fusion.69 = f32[16,512,72]{1,2,0:T(8,128)} fusion(f32[16,512,72]{1,2,0:T(8,128)} %get-tuple-element.185, f32[16,512,512]{2,1,0:T(8,128)} %get-tuple-element.170, f32[16,512]{1,0:T(8,128)S(1)} %select_maximum_fusion.2, bf16[8,512,16,72]{1,3,2,0:T(8,128)(2,1)} %get-tuple-element.197, s32[]{:T(128)} %get-tuple-element.182, ...), kind=kOutput, calls=%fused_computation.13.clone.1 | convolution fusion | flops 618332160 | bytes 22741504 | tf_op jit(solution)/shard_map/while/body/eval_jaxpr/hqk,khe->hqe/dot_general | solution.py:90
  601.0 9.7 %bitcast_reduce_fusion.2 = (f32[16,512]{1,0:T(8,128)S(1)}, f32[16,512,512]{2,1,0:T(8,128)}) fusion(bf16[512,16,72]{0,2,1:T(8,128)(2,1)} %get-tuple-element.196, bf16[8,512,16,72]{1,3,2,0:T(8,128)(2,1)} %get-tuple-element.195, s32[]{:T(128)} %get-tuple-element.182), kind=kOutput, calls=%fused_computation.5.clone.1 | convolution fusion | flops 612360192 | bytes 19169792 | tf_op jit(solution)/shard_map/while/body/eval_jaxpr/qhe,khe->hqk/dot_general | solution.py:83
  619.3 11.1 %fusion.69 = f32[16,512,72]{1,2,0:T(8,128)} fusion(f32[16,512,72]{1,2,0:T(8,128)} %get-tuple-element.185, f32[16,512,512]{2,1,0:T(8,128)} %get-tuple-element.170, f32[16,512]{1,0:T(8,128)S(1)} %select_maximum_fusion.2, bf16[8,512,16,72]{1,3,2,0:T(8,128)(2,1)} %get-tuple-element.197, s32[]{:T(128)} %get-tuple-element.182, ...), kind=kOutput, calls=%fused_computation.13.clone.1 | convolution fusion | flops 618332160 | bytes 22741504 | tf_op jit(solution)/shard_map/while/body/eval_jaxpr/hqk,khe->hqe/dot_general | solution.py:90
  630.4 9.7 %bitcast_reduce_fusion.2 = (f32[16,512]{1,0:T(8,128)S(1)}, f32[16,512,512]{2,1,0:T(8,128)}) fusion(bf16[512,16,72]{0,2,1:T(8,128)(2,1)} %get-tuple-element.196, bf16[8,512,16,72]{1,3,2,0:T(8,128)(2,1)} %get-tuple-element.195, s32[]{:T(128)} %get-tuple-element.182), kind=kOutput, calls=%fused_computation.5.clone.1 | convolution fusion | flops 612360192 | bytes 19169792 | tf_op jit(solution)/shard_map/while/body/eval_jaxpr/qhe,khe->hqk/dot_general | solution.py:83
  640.2 8.6 %fusion.67 = f32[16,512]{1,0:T(8,128)S(1)} fusion(f32[16,512,512]{2,1,0:T(8,128)} %get-tuple-element.170, f32[16,512]{1,0:T(8,128)S(1)} %select_maximum_fusion.2), kind=kLoop, calls=%fused_computation.8.clone.1 | loop fusion | flops 12574720 | bytes 16842752 | tf_op jit(solution)/shard_map/while/body/eval_jaxpr/reduce_sum | solution.py:89
  648.8 11.1 %fusion.69 = f32[16,512,72]{1,2,0:T(8,128)} fusion(f32[16,512,72]{1,2,0:T(8,128)} %get-tuple-element.185, f32[16,512,512]{2,1,0:T(8,128)} %get-tuple-element.170, f32[16,512]{1,0:T(8,128)S(1)} %select_maximum_fusion.2, bf16[8,512,16,72]{1,3,2,0:T(8,128)(2,1)} %get-tuple-element.197, s32[]{:T(128)} %get-tuple-element.182, ...), kind=kOutput, calls=%fused_computation.13.clone.1 | convolution fusion | flops 618332160 | bytes 22741504 | tf_op jit(solution)/shard_map/while/body/eval_jaxpr/hqk,khe->hqe/dot_general | solution.py:90
  659.9 9.7 %bitcast_reduce_fusion.2 = (f32[16,512]{1,0:T(8,128)S(1)}, f32[16,512,512]{2,1,0:T(8,128)}) fusion(bf16[512,16,72]{0,2,1:T(8,128)(2,1)} %get-tuple-element.196, bf16[8,512,16,72]{1,3,2,0:T(8,128)(2,1)} %get-tuple-element.195, s32[]{:T(128)} %get-tuple-element.182), kind=kOutput, calls=%fused_computation.5.clone.1 | convolution fusion | flops 612360192 | bytes 19169792 | tf_op jit(solution)/shard_map/while/body/eval_jaxpr/qhe,khe->hqk/dot_general | solution.py:83
  669.6 8.6 %fusion.67 = f32[16,512]{1,0:T(8,128)S(1)} fusion(f32[16,512,512]{2,1,0:T(8,128)} %get-tuple-element.170, f32[16,512]{1,0:T(8,128)S(1)} %select_maximum_fusion.2), kind=kLoop, calls=%fused_computation.8.clone.1 | loop fusion | flops 12574720 | bytes 16842752 | tf_op jit(solution)/shard_map/while/body/eval_jaxpr/reduce_sum | solution.py:89
  678.2 11.1 %fusion.69 = f32[16,512,72]{1,2,0:T(8,128)} fusion(f32[16,512,72]{1,2,0:T(8,128)} %get-tuple-element.185, f32[16,512,512]{2,1,0:T(8,128)} %get-tuple-element.170, f32[16,512]{1,0:T(8,128)S(1)} %select_maximum_fusion.2, bf16[8,512,16,72]{1,3,2,0:T(8,128)(2,1)} %get-tuple-element.197, s32[]{:T(128)} %get-tuple-element.182, ...), kind=kOutput, calls=%fused_computation.13.clone.1 | convolution fusion | flops 618332160 | bytes 22741504 | tf_op jit(solution)/shard_map/while/body/eval_jaxpr/hqk,khe->hqe/dot_general | solution.py:90
  689.3 9.7 %bitcast_reduce_fusion.2 = (f32[16,512]{1,0:T(8,128)S(1)}, f32[16,512,512]{2,1,0:T(8,128)}) fusion(bf16[512,16,72]{0,2,1:T(8,128)(2,1)} %get-tuple-element.196, bf16[8,512,16,72]{1,3,2,0:T(8,128)(2,1)} %get-tuple-element.195, s32[]{:T(128)} %get-tuple-element.182), kind=kOutput, calls=%fused_computation.5.clone.1 | convolution fusion | flops 612360192 | bytes 19169792 | tf_op jit(solution)/shard_map/while/body/eval_jaxpr/qhe,khe->hqk/dot_general | solution.py:83
  699.0 8.6 %fusion.67 = f32[16,512]{1,0:T(8,128)S(1)} fusion(f32[16,512,512]{2,1,0:T(8,128)} %get-tuple-element.170, f32[16,512]{1,0:T(8,128)S(1)} %select_maximum_fusion.2), kind=kLoop, calls=%fused_computation.8.clone.1 | loop fusion | flops 12574720 | bytes 16842752 | tf_op jit(solution)/shard_map/while/body/eval_jaxpr/reduce_sum | solution.py:89
  707.6 11.1 %fusion.69 = f32[16,512,72]{1,2,0:T(8,128)} fusion(f32[16,512,72]{1,2,0:T(8,128)} %get-tuple-element.185, f32[16,512,512]{2,1,0:T(8,128)} %get-tuple-element.170, f32[16,512]{1,0:T(8,128)S(1)} %select_maximum_fusion.2, bf16[8,512,16,72]{1,3,2,0:T(8,128)(2,1)} %get-tuple-element.197, s32[]{:T(128)} %get-tuple-element.182, ...), kind=kOutput, calls=%fused_computation.13.clone.1 | convolution fusion | flops 618332160 | bytes 22741504 | tf_op jit(solution)/shard_map/while/body/eval_jaxpr/hqk,khe->hqe/dot_general | solution.py:90
  718.7 9.7 %bitcast_reduce_fusion.2 = (f32[16,512]{1,0:T(8,128)S(1)}, f32[16,512,512]{2,1,0:T(8,128)}) fusion(bf16[512,16,72]{0,2,1:T(8,128)(2,1)} %get-tuple-element.196, bf16[8,512,16,72]{1,3,2,0:T(8,128)(2,1)} %get-tuple-element.195, s32[]{:T(128)} %get-tuple-element.182), kind=kOutput, calls=%fused_computation.5.clone.1 | convolution fusion | flops 612360192 | bytes 19169792 | tf_op jit(solution)/shard_map/while/body/eval_jaxpr/qhe,khe->hqk/dot_general | solution.py:83
  728.5 8.6 %fusion.67 = f32[16,512]{1,0:T(8,128)S(1)} fusion(f32[16,512,512]{2,1,0:T(8,128)} %get-tuple-element.170, f32[16,512]{1,0:T(8,128)S(1)} %select_maximum_fusion.2), kind=kLoop, calls=%fused_computation.8.clone.1 | loop fusion | flops 12574720 | bytes 16842752 | tf_op jit(solution)/shard_map/while/body/eval_jaxpr/reduce_sum | solution.py:89
  737.1 11.1 %fusion.69 = f32[16,512,72]{1,2,0:T(8,128)} fusion(f32[16,512,72]{1,2,0:T(8,128)} %get-tuple-element.185, f32[16,512,512]{2,1,0:T(8,128)} %get-tuple-element.170, f32[16,512]{1,0:T(8,128)S(1)} %select_maximum_fusion.2, bf16[8,512,16,72]{1,3,2,0:T(8,128)(2,1)} %get-tuple-element.197, s32[]{:T(128)} %get-tuple-element.182, ...), kind=kOutput, calls=%fused_computation.13.clone.1 | convolution fusion | flops 618332160 | bytes 22741504 | tf_op jit(solution)/shard_map/while/body/eval_jaxpr/hqk,khe->hqe/dot_general | solution.py:90
  748.1 9.7 %bitcast_reduce_fusion.2 = (f32[16,512]{1,0:T(8,128)S(1)}, f32[16,512,512]{2,1,0:T(8,128)}) fusion(bf16[512,16,72]{0,2,1:T(8,128)(2,1)} %get-tuple-element.196, bf16[8,512,16,72]{1,3,2,0:T(8,128)(2,1)} %get-tuple-element.195, s32[]{:T(128)} %get-tuple-element.182), kind=kOutput, calls=%fused_computation.5.clone.1 | convolution fusion | flops 612360192 | bytes 19169792 | tf_op jit(solution)/shard_map/while/body/eval_jaxpr/qhe,khe->hqk/dot_general | solution.py:83
  766.5 11.1 %fusion.69 = f32[16,512,72]{1,2,0:T(8,128)} fusion(f32[16,512,72]{1,2,0:T(8,128)} %get-tuple-element.185, f32[16,512,512]{2,1,0:T(8,128)} %get-tuple-element.170, f32[16,512]{1,0:T(8,128)S(1)} %select_maximum_fusion.2, bf16[8,512,16,72]{1,3,2,0:T(8,128)(2,1)} %get-tuple-element.197, s32[]{:T(128)} %get-tuple-element.182, ...), kind=kOutput, calls=%fused_computation.13.clone.1 | convolution fusion | flops 618332160 | bytes 22741504 | tf_op jit(solution)/shard_map/while/body/eval_jaxpr/hqk,khe->hqe/dot_general | solution.py:90
  (75 shorter events, 71.6 us)
Async XLA Ops:
  6.5 773.1 %copy-start = (bf16[1152,1152]{1,0:T(8,128)(2,1)S(1)}, bf16[1152,1152]{1,0:T(8,128)(2,1)}, u32[]{:S(2)}) copy-start(bf16[1152,1152]{1,0:T(8,128)(2,1)} %param.19) | copy-start | bytes 7962628
  6.5 30.5 %copy-start.1 = (bf16[128,1152]{1,0:T(8,128)(2,1)S(1)}, bf16[128,1152]{1,0:T(8,128)(2,1)}, u32[]{:S(2)}) copy-start(bf16[128,1152]{1,0:T(8,128)(2,1)} %param.15) | copy-start | bytes 884740
  44.6 38.4 %all-to-all-start.1 = ((bf16[128,6,1152]{2,1,0:T(8,128)(2,1)}), bf16[128,6,1152]{2,1,0:T(8,128)(2,1)}, u32[]{:S(2)}, u32[]{:S(2)}) async-start(bf16[128,6,1152]{2,1,0:T(8,128)(2,1)} %reshape.223), calls=%async_computation.1 | async-start | bytes 4718592 | tf_op jit(solution)/shard_map/all_to_all | solution.py:50
  49.9 247.6 %all-gather.3.cloned.1.call-start = ((), (), s32[]{:S(2)}) async-start(), calls=%async_computation.2 | async-start | bytes 10616832 | tf_op jit(solution)/shard_map/all_gather | solution.py:72
  86.9 5.4 copy-start.4
  92.3 8.0 %copy-start.2 = (bf16[1,512,1152]{2,1,0:T(8,128)(2,1)S(1)}, bf16[1,512,1152]{2,1,0:T(8,128)(2,1)}, u32[]{:S(2)}) copy-start(bf16[1,512,1152]{2,1,0:T(8,128)(2,1)} %param.11) | copy-start | bytes 3538948
  100.3 11.5 %copy-start.5 = (f32[512,3456]{1,0:T(8,128)}, f32[512,3456]{1,0:T(8,128)S(1)}, u32[]{:S(2)}) copy-start(f32[512,3456]{1,0:T(8,128)S(1)} %fusion.19) | copy-start | bytes 21233668
  113.7 374.5 %all-gather.5.cloned.1.call-start = ((), (), s32[]{:S(2)}) async-start(), calls=%async_computation.3 | async-start | bytes 10616832 | tf_op jit(solution)/shard_map/all_gather | solution.py:73
  777.6 2.1 copy-start.3
Sparse Core Ops, SparseCore 0:
  113.9 183.5 all-gather.2
  299.1 189.0 all-gather.4
where the time goes:
time: 794 us; the launch traced here: 791 us
  waiting for transfers between devices  347 us (44%)
  matrix products  190 us (24%)
  local copies, waits for them, and re-layouts  137 us (17%)
  other arithmetic  76 us (10%)
  blocking collectives  21 us (3%)
  between operations  14.2 us (2%)
    all_gather x1, waiting for transfers between devices, per_device(): keys_piece = lax.all_gather(keys_here, 'ctx', axis=0, tiled=True)  181 us
    all_gather x1, waiting for transfers between devices, per_device(): values_piece = lax.all_gather(values_here, 'ctx', axis=0, tiled=True)  136 us
    dot_general x8, matrix products, advance(): jnp.einsum('hqk,khe->hqe', expo.astype(jnp.bfloat16), value_block, prefer...  88 us
    dot_general x8, matrix products, advance(): jnp.einsum('qhe,khe->hqk', query_heads, key_block, preferred_element_type...  77.9 us
    reduce_sum x8, other arithmetic, advance(): denominator = denominator * shrink + jnp.sum(expo, axis=2)  68.4 us
    unnamed x14, local copies, waits for them, and re-layouts  43 us
    reshape x1, local copies, waits for them, and re-layouts, per_device(): values_piece.reshape(piece_rows // block_rows, block_rows, HEADS, head_dim)  33.2 us
    reshape x1, local copies, waits for them, and re-layouts, per_device(): keys_piece.reshape(piece_rows // block_rows, block_rows, HEADS, head_dim)  33.2 us
  transfers between devices with their start and end apart: 3, of which 3 were waited for; matrix products, arithmetic and copies ran while one was open for 8% of the time, Pallas kernels for 0%

commit v1 on v0

--- a/solution.py
+++ b/solution.py
@@ -69,8 +69,13 @@
         jnp.zeros((HEADS, tok_rows), jnp.float32),
         jnp.zeros((HEADS, tok_rows, head_dim), jnp.float32),
     )
-    keys_piece = lax.all_gather(keys_here, "ctx", axis=0, tiled=True)
-    values_piece = lax.all_gather(values_here, "ctx", axis=0, tiled=True)
+    keys_piece, values_piece = jnp.split(
+        lax.all_gather(
+            jnp.concatenate([keys_here, values_here], axis=1), "ctx", axis=0, tiled=True
+        ),
+        [keys_here.shape[1]],
+        axis=1,
+    )
     piece_rows = keys_piece.shape[0]
     block_rows = math.gcd(piece_rows, 512)
     key_blocks = keys_piece.reshape(piece_rows // block_rows, block_rows, HEADS, head_dim)

time: 794 us -> 851 us (1.072)
  waiting for transfers between devices: 347 us -> 385 us
  local copies, waits for them, and re-layouts: 137 us -> 156 us
    all_gather x2 -> x1, waiting for transfers between devices: 317 us -> 356 us  [per_device(): lax.all_gather(jnp.concatenate([keys_here, values_here], axis=1), 'ctx',...]
    split x0 -> x1, local copies, waits for them, and re-layouts: none -> 14.6 us  [per_device(): jnp.split(lax.all_gather(jnp.concatenate([keys_here, values_here], axis=1...]
    unnamed x14 -> x16, local copies, waits for them, and re-layouts: 43 us -> 44.7 us
  transfers between devices with their start and end apart: 3 -> 2, of which waited for: 3 -> 2; matrix products, arithmetic and copies ran while one was open for 8% -> 1% of each run, Pallas kernels for 0% -> 0%
where the time goes in v1:
time: 851 us; the launch traced here: 848 us
  waiting for transfers between devices  385 us (45%)
  matrix products  190 us (22%)
  local copies, waits for them, and re-layouts  156 us (18%)
  other arithmetic  76 us (9%)
  blocking collectives  21 us (2%)
  between operations  14.2 us (2%)
    all_gather x1, waiting for transfers between devices, per_device(): lax.all_gather(jnp.concatenate([keys_here, values_here], axis=1), 'ctx',...  356 us
    dot_general x8, matrix products, advance(): jnp.einsum('hqk,khe->hqe', expo.astype(jnp.bfloat16), value_block, prefer...  88.2 us
    dot_general x8, matrix products, advance(): jnp.einsum('qhe,khe->hqk', query_heads, key_block, preferred_element_type...  77.9 us
    reduce_sum x8, other arithmetic, advance(): denominator = denominator * shrink + jnp.sum(expo, axis=2)  68.4 us
    unnamed x16, local copies, waits for them, and re-layouts  44.7 us
    reshape x1, local copies, waits for them, and re-layouts, per_device(): keys_piece.reshape(piece_rows // block_rows, block_rows, HEADS, head_dim)  33.2 us
    reshape x1, local copies, waits for them, and re-layouts, per_device(): values_piece.reshape(piece_rows // block_rows, block_rows, HEADS, head_dim)  33.2 us
    all_to_all x1, waiting for transfers between devices, per_device(): lax.all_to_all(served, ('region', 'ctx'), split_axis=0, concat_axis=0, ti...  29.6 us
  transfers between devices with their start and end apart: 2, of which 2 were waited for; matrix products, arithmetic and copies ran while one was open for 1% of the time, Pallas kernels for 0%

profile of v1, /device:TPU:1, one launch (start us, length us, event | category | flops | bytes accessed | tf_op | source)
XLA Modules:
  0.0 848.2 jit_solution(14959123706047776104)
XLA Ops:
  14.5 21.0 %all_to_all.14 = s32[128,1,6]{2,1,0:T(1,128)S(1)} all-to-all(s32[128,1,6]{2,1,0:T(1,128)S(1)} %bitcast.77), channel_id=1, replica_groups=mesh['region'=16,'ctx'=8] {'region','ctx'}, dimensions={0} | all-to-all | bytes 6144 | tf_op jit(solution)/shard_map/all_to_all | solution.py:41
  53.4 29.6 %all-to-all-done.1 = bf16[128,6,1152]{2,1,0:T(8,128)(2,1)} async-done(((bf16[128,6,1152]{2,1,0:T(8,128)(2,1)}), bf16[128,6,1152]{2,1,0:T(8,128)(2,1)}, u32[]{:S(2)}, u32[]{:S(2)}) %all-to-all-start.1) | async-done | bytes 1769504 | tf_op jit(solution)/shard_map/all_to_all | solution.py:50
  100.3 11.4 %convolution_convert_fusion = bf16[512,3456]{1,0:T(8,128)(2,1)S(1)} fusion(bf16[1152,3456]{1,0:T(8,128)(2,1)} %param.18, bf16[1,512,1152]{2,1,0:T(8,128)(2,1)S(1)} %copy-done.2, f32[512,3456]{1,0:T(8,128)S(1)} %fusion.19, f32[512]{0:T(512)S(1)} %add_rsqrt_fusion, f32[512]{0:T(512)S(1)} %broadcast_multiply_fusion), kind=kOutput, calls=%fused_computation.28 | convolution fusion | flops 4082761728 | bytes 17403904 | tf_op jit(solution)/shard_map/dot_general | solution.py:60
  120.0 355.9 %all-gather.2.cloned.1.call-done = bf16[4096,2304]{1,0:T(8,128)(2,1)} async-done(((bf16[512,2304]{1,0:T(8,128)(2,1)}), bf16[4096,2304]{1,0:T(8,128)(2,1)}) %all-gather.2.cloned.1.call-update) | async-done | bytes 18874384 | tf_op jit(solution)/shard_map/all_gather | solution.py:73
  475.9 14.6 %fusion.52 = (bf16[4096,1152]{1,0:T(8,128)(2,1)}, bf16[4096,1152]{1,0:T(8,128)(2,1)}) fusion(bf16[4096,2304]{1,0:T(8,128)(2,1)} %all-gather.2.cloned.1.call-done), kind=kLoop, calls=%fused_computation.90 | loop fusion | bytes 37748736 | tf_op jit(solution)/shard_map/split | solution.py:72
  490.5 33.2 %reshape.260 = bf16[8,512,16,72]{3,2,1,0:T(8,128)(2,1)} reshape(bf16[4096,1152]{1,0:T(8,128)(2,1)} %get-tuple-element.118) | data formatting | bytes 18874368 | tf_op jit(solution)/shard_map/reshape | solution.py:81
  523.7 21.4 %copy.32 = bf16[8,512,16,72]{1,3,2,0:T(8,128)(2,1)} copy(bf16[8,512,16,72]{3,2,1,0:T(8,128)(2,1)} %reshape.260) | data formatting | bytes 18874368
  545.1 33.2 %reshape.261 = bf16[8,512,16,72]{3,2,1,0:T(8,128)(2,1)} reshape(bf16[4096,1152]{1,0:T(8,128)(2,1)} %get-tuple-element.117) | data formatting | bytes 18874368 | tf_op jit(solution)/shard_map/reshape | solution.py:82
  578.3 21.4 %copy.33 = bf16[8,512,16,72]{1,3,2,0:T(8,128)(2,1)} copy(bf16[8,512,16,72]{3,2,1,0:T(8,128)(2,1)} %reshape.261) | data formatting | bytes 18874368
  599.7 234.9 %while.15 = (s32[]{:T(128)}, f32[16,512]{1,0:T(8,128)S(1)}, f32[16,512]{1,0:T(8,128)S(1)}, f32[16,512,72]{1,2,0:T(8,128)}, bf16[8,512,16,72]{1,3,2,0:T(8,128)(2,...) while((s32[]{:T(128)}, f32[16,512]{1,0:T(8,128)S(1)}, ...), condition=%wide.region_7.8_spmd.clone, body=%wide.region_4.7_spmd.clone.sunk | while | flops 1243324416 | bytes 59114596 | solution.py:103
  599.7 9.7 %bitcast_reduce_fusion.2 = (f32[16,512]{1,0:T(8,128)S(1)}, f32[16,512,512]{2,1,0:T(8,128)}) fusion(bf16[512,16,72]{0,2,1:T(8,128)(2,1)} %get-tuple-element.195, bf16[8,512,16,72]{1,3,2,0:T(8,128)(2,1)} %get-tuple-element.194, s32[]{:T(128)} %get-tuple-element.181), kind=kOutput, calls=%fused_computation.5.clone.1 | convolution fusion | flops 612360192 | bytes 19169792 | tf_op jit(solution)/shard_map/while/body/eval_jaxpr/qhe,khe->hqk/dot_general | solution.py:88
  609.5 8.6 %fusion.67 = f32[16,512]{1,0:T(8,128)S(1)} fusion(f32[16,512,512]{2,1,0:T(8,128)} %get-tuple-element.169, f32[16,512]{1,0:T(8,128)S(1)} %select_maximum_fusion.2), kind=kLoop, calls=%fused_computation.8.clone.1 | loop fusion | flops 12574720 | bytes 16842752 | tf_op jit(solution)/shard_map/while/body/eval_jaxpr/reduce_sum | solution.py:94
  618.1 10.4 %fusion.69 = f32[16,512,72]{1,2,0:T(8,128)} fusion(f32[16,512,72]{1,2,0:T(8,128)} %get-tuple-element.184, f32[16,512,512]{2,1,0:T(8,128)} %get-tuple-element.169, f32[16,512]{1,0:T(8,128)S(1)} %select_maximum_fusion.2, bf16[8,512,16,72]{1,3,2,0:T(8,128)(2,1)} %get-tuple-element.196, s32[]{:T(128)} %get-tuple-element.181, ...), kind=kOutput, calls=%fused_computation.13.clone.1 | convolution fusion | flops 618332160 | bytes 22741504 | tf_op jit(solution)/shard_map/while/body/eval_jaxpr/hqk,khe->hqe/dot_general | solution.py:95
  628.5 9.7 %bitcast_reduce_fusion.2 = (f32[16,512]{1,0:T(8,128)S(1)}, f32[16,512,512]{2,1,0:T(8,128)}) fusion(bf16[512,16,72]{0,2,1:T(8,128)(2,1)} %get-tuple-element.195, bf16[8,512,16,72]{1,3,2,0:T(8,128)(2,1)} %get-tuple-element.194, s32[]{:T(128)} %get-tuple-element.181), kind=kOutput, calls=%fused_computation.5.clone.1 | convolution fusion | flops 612360192 | bytes 19169792 | tf_op jit(solution)/shard_map/while/body/eval_jaxpr/qhe,khe->hqk/dot_general | solution.py:88
  638.2 8.6 %fusion.67 = f32[16,512]{1,0:T(8,128)S(1)} fusion(f32[16,512,512]{2,1,0:T(8,128)} %get-tuple-element.169, f32[16,512]{1,0:T(8,128)S(1)} %select_maximum_fusion.2), kind=kLoop, calls=%fused_computation.8.clone.1 | loop fusion | flops 12574720 | bytes 16842752 | tf_op jit(solution)/shard_map/while/body/eval_jaxpr/reduce_sum | solution.py:94
  646.8 11.1 %fusion.69 = f32[16,512,72]{1,2,0:T(8,128)} fusion(f32[16,512,72]{1,2,0:T(8,128)} %get-tuple-element.184, f32[16,512,512]{2,1,0:T(8,128)} %get-tuple-element.169, f32[16,512]{1,0:T(8,128)S(1)} %select_maximum_fusion.2, bf16[8,512,16,72]{1,3,2,0:T(8,128)(2,1)} %get-tuple-element.196, s32[]{:T(128)} %get-tuple-element.181, ...), kind=kOutput, calls=%fused_computation.13.clone.1 | convolution fusion | flops 618332160 | bytes 22741504 | tf_op jit(solution)/shard_map/while/body/eval_jaxpr/hqk,khe->hqe/dot_general | solution.py:95
  657.9 9.7 %bitcast_reduce_fusion.2 = (f32[16,512]{1,0:T(8,128)S(1)}, f32[16,512,512]{2,1,0:T(8,128)}) fusion(bf16[512,16,72]{0,2,1:T(8,128)(2,1)} %get-tuple-element.195, bf16[8,512,16,72]{1,3,2,0:T(8,128)(2,1)} %get-tuple-element.194, s32[]{:T(128)} %get-tuple-element.181), kind=kOutput, calls=%fused_computation.5.clone.1 | convolution fusion | flops 612360192 | bytes 19169792 | tf_op jit(solution)/shard_map/while/body/eval_jaxpr/qhe,khe->hqk/dot_general | solution.py:88
  667.7 8.6 %fusion.67 = f32[16,512]{1,0:T(8,128)S(1)} fusion(f32[16,512,512]{2,1,0:T(8,128)} %get-tuple-element.169, f32[16,512]{1,0:T(8,128)S(1)} %select_maximum_fusion.2), kind=kLoop, calls=%fused_computation.8.clone.1 | loop fusion | flops 12574720 | bytes 16842752 | tf_op jit(solution)/shard_map/while/body/eval_jaxpr/reduce_sum | solution.py:94
  676.3 11.1 %fusion.69 = f32[16,512,72]{1,2,0:T(8,128)} fusion(f32[16,512,72]{1,2,0:T(8,128)} %get-tuple-element.184, f32[16,512,512]{2,1,0:T(8,128)} %get-tuple-element.169, f32[16,512]{1,0:T(8,128)S(1)} %select_maximum_fusion.2, bf16[8,512,16,72]{1,3,2,0:T(8,128)(2,1)} %get-tuple-element.196, s32[]{:T(128)} %get-tuple-element.181, ...), kind=kOutput, calls=%fused_computation.13.clone.1 | convolution fusion | flops 618332160 | bytes 22741504 | tf_op jit(solution)/shard_map/while/body/eval_jaxpr/hqk,khe->hqe/dot_general | solution.py:95
  687.4 9.7 %bitcast_reduce_fusion.2 = (f32[16,512]{1,0:T(8,128)S(1)}, f32[16,512,512]{2,1,0:T(8,128)}) fusion(bf16[512,16,72]{0,2,1:T(8,128)(2,1)} %get-tuple-element.195, bf16[8,512,16,72]{1,3,2,0:T(8,128)(2,1)} %get-tuple-element.194, s32[]{:T(128)} %get-tuple-element.181), kind=kOutput, calls=%fused_computation.5.clone.1 | convolution fusion | flops 612360192 | bytes 19169792 | tf_op jit(solution)/shard_map/while/body/eval_jaxpr/qhe,khe->hqk/dot_general | solution.py:88
  705.7 11.1 %fusion.69 = f32[16,512,72]{1,2,0:T(8,128)} fusion(f32[16,512,72]{1,2,0:T(8,128)} %get-tuple-element.184, f32[16,512,512]{2,1,0:T(8,128)} %get-tuple-element.169, f32[16,512]{1,0:T(8,128)S(1)} %select_maximum_fusion.2, bf16[8,512,16,72]{1,3,2,0:T(8,128)(2,1)} %get-tuple-element.196, s32[]{:T(128)} %get-tuple-element.181, ...), kind=kOutput, calls=%fused_computation.13.clone.1 | convolution fusion | flops 618332160 | bytes 22741504 | tf_op jit(solution)/shard_map/while/body/eval_jaxpr/hqk,khe->hqe/dot_general | solution.py:95
  716.8 9.7 %bitcast_reduce_fusion.2 = (f32[16,512]{1,0:T(8,128)S(1)}, f32[16,512,512]{2,1,0:T(8,128)}) fusion(bf16[512,16,72]{0,2,1:T(8,128)(2,1)} %get-tuple-element.195, bf16[8,512,16,72]{1,3,2,0:T(8,128)(2,1)} %get-tuple-element.194, s32[]{:T(128)} %get-tuple-element.181), kind=kOutput, calls=%fused_computation.5.clone.1 | convolution fusion | flops 612360192 | bytes 19169792 | tf_op jit(solution)/shard_map/while/body/eval_jaxpr/qhe,khe->hqk/dot_general | solution.py:88
  726.6 8.6 %fusion.67 = f32[16,512]{1,0:T(8,128)S(1)} fusion(f32[16,512,512]{2,1,0:T(8,128)} %get-tuple-element.169, f32[16,512]{1,0:T(8,128)S(1)} %select_maximum_fusion.2), kind=kLoop, calls=%fused_computation.8.clone.1 | loop fusion | flops 12574720 | bytes 16842752 | tf_op jit(solution)/shard_map/while/body/eval_jaxpr/reduce_sum | solution.py:94
  735.2 11.1 %fusion.69 = f32[16,512,72]{1,2,0:T(8,128)} fusion(f32[16,512,72]{1,2,0:T(8,128)} %get-tuple-element.184, f32[16,512,512]{2,1,0:T(8,128)} %get-tuple-element.169, f32[16,512]{1,0:T(8,128)S(1)} %select_maximum_fusion.2, bf16[8,512,16,72]{1,3,2,0:T(8,128)(2,1)} %get-tuple-element.196, s32[]{:T(128)} %get-tuple-element.181, ...), kind=kOutput, calls=%fused_computation.13.clone.1 | convolution fusion | flops 618332160 | bytes 22741504 | tf_op jit(solution)/shard_map/while/body/eval_jaxpr/hqk,khe->hqe/dot_general | solution.py:95
  746.3 9.7 %bitcast_reduce_fusion.2 = (f32[16,512]{1,0:T(8,128)S(1)}, f32[16,512,512]{2,1,0:T(8,128)}) fusion(bf16[512,16,72]{0,2,1:T(8,128)(2,1)} %get-tuple-element.195, bf16[8,512,16,72]{1,3,2,0:T(8,128)(2,1)} %get-tuple-element.194, s32[]{:T(128)} %get-tuple-element.181), kind=kOutput, calls=%fused_computation.5.clone.1 | convolution fusion | flops 612360192 | bytes 19169792 | tf_op jit(solution)/shard_map/while/body/eval_jaxpr/qhe,khe->hqk/dot_general | solution.py:88
  764.6 11.1 %fusion.69 = f32[16,512,72]{1,2,0:T(8,128)} fusion(f32[16,512,72]{1,2,0:T(8,128)} %get-tuple-element.184, f32[16,512,512]{2,1,0:T(8,128)} %get-tuple-element.169, f32[16,512]{1,0:T(8,128)S(1)} %select_maximum_fusion.2, bf16[8,512,16,72]{1,3,2,0:T(8,128)(2,1)} %get-tuple-element.196, s32[]{:T(128)} %get-tuple-element.181, ...), kind=kOutput, calls=%fused_computation.13.clone.1 | convolution fusion | flops 618332160 | bytes 22741504 | tf_op jit(solution)/shard_map/while/body/eval_jaxpr/hqk,khe->hqe/dot_general | solution.py:95
  775.7 9.7 %bitcast_reduce_fusion.2 = (f32[16,512]{1,0:T(8,128)S(1)}, f32[16,512,512]{2,1,0:T(8,128)}) fusion(bf16[512,16,72]{0,2,1:T(8,128)(2,1)} %get-tuple-element.195, bf16[8,512,16,72]{1,3,2,0:T(8,128)(2,1)} %get-tuple-element.194, s32[]{:T(128)} %get-tuple-element.181), kind=kOutput, calls=%fused_computation.5.clone.1 | convolution fusion | flops 612360192 | bytes 19169792 | tf_op jit(solution)/shard_map/while/body/eval_jaxpr/qhe,khe->hqk/dot_general | solution.py:88
  785.5 8.6 %fusion.67 = f32[16,512]{1,0:T(8,128)S(1)} fusion(f32[16,512,512]{2,1,0:T(8,128)} %get-tuple-element.169, f32[16,512]{1,0:T(8,128)S(1)} %select_maximum_fusion.2), kind=kLoop, calls=%fused_computation.8.clone.1 | loop fusion | flops 12574720 | bytes 16842752 | tf_op jit(solution)/shard_map/while/body/eval_jaxpr/reduce_sum | solution.py:94
  794.1 11.1 %fusion.69 = f32[16,512,72]{1,2,0:T(8,128)} fusion(f32[16,512,72]{1,2,0:T(8,128)} %get-tuple-element.184, f32[16,512,512]{2,1,0:T(8,128)} %get-tuple-element.169, f32[16,512]{1,0:T(8,128)S(1)} %select_maximum_fusion.2, bf16[8,512,16,72]{1,3,2,0:T(8,128)(2,1)} %get-tuple-element.196, s32[]{:T(128)} %get-tuple-element.181, ...), kind=kOutput, calls=%fused_computation.13.clone.1 | convolution fusion | flops 618332160 | bytes 22741504 | tf_op jit(solution)/shard_map/while/body/eval_jaxpr/hqk,khe->hqe/dot_general | solution.py:95
  805.2 9.7 %bitcast_reduce_fusion.2 = (f32[16,512]{1,0:T(8,128)S(1)}, f32[16,512,512]{2,1,0:T(8,128)}) fusion(bf16[512,16,72]{0,2,1:T(8,128)(2,1)} %get-tuple-element.195, bf16[8,512,16,72]{1,3,2,0:T(8,128)(2,1)} %get-tuple-element.194, s32[]{:T(128)} %get-tuple-element.181), kind=kOutput, calls=%fused_computation.5.clone.1 | convolution fusion | flops 612360192 | bytes 19169792 | tf_op jit(solution)/shard_map/while/body/eval_jaxpr/qhe,khe->hqk/dot_general | solution.py:88
  814.9 8.6 %fusion.67 = f32[16,512]{1,0:T(8,128)S(1)} fusion(f32[16,512,512]{2,1,0:T(8,128)} %get-tuple-element.169, f32[16,512]{1,0:T(8,128)S(1)} %select_maximum_fusion.2), kind=kLoop, calls=%fused_computation.8.clone.1 | loop fusion | flops 12574720 | bytes 16842752 | tf_op jit(solution)/shard_map/while/body/eval_jaxpr/reduce_sum | solution.py:94
  823.5 11.1 %fusion.69 = f32[16,512,72]{1,2,0:T(8,128)} fusion(f32[16,512,72]{1,2,0:T(8,128)} %get-tuple-element.184, f32[16,512,512]{2,1,0:T(8,128)} %get-tuple-element.169, f32[16,512]{1,0:T(8,128)S(1)} %select_maximum_fusion.2, bf16[8,512,16,72]{1,3,2,0:T(8,128)(2,1)} %get-tuple-element.196, s32[]{:T(128)} %get-tuple-element.181, ...), kind=kOutput, calls=%fused_computation.13.clone.1 | convolution fusion | flops 618332160 | bytes 22741504 | tf_op jit(solution)/shard_map/while/body/eval_jaxpr/hqk,khe->hqe/dot_general | solution.py:95
  (76 shorter events, 74.7 us)
Async XLA Ops:
  6.5 830.2 %copy-start = (bf16[1152,1152]{1,0:T(8,128)(2,1)S(1)}, bf16[1152,1152]{1,0:T(8,128)(2,1)}, u32[]{:S(2)}) copy-start(bf16[1152,1152]{1,0:T(8,128)(2,1)} %param.19) | copy-start | bytes 7962628
  6.5 30.5 %copy-start.1 = (bf16[128,1152]{1,0:T(8,128)(2,1)S(1)}, bf16[128,1152]{1,0:T(8,128)(2,1)}, u32[]{:S(2)}) copy-start(bf16[128,1152]{1,0:T(8,128)(2,1)} %param.15) | copy-start | bytes 884740
  44.6 38.4 %all-to-all-start.1 = ((bf16[128,6,1152]{2,1,0:T(8,128)(2,1)}), bf16[128,6,1152]{2,1,0:T(8,128)(2,1)}, u32[]{:S(2)}, u32[]{:S(2)}) async-start(bf16[128,6,1152]{2,1,0:T(8,128)(2,1)} %reshape.223), calls=%async_computation.1 | async-start | bytes 4718592 | tf_op jit(solution)/shard_map/all_to_all | solution.py:50
  49.9 426.0 %all-gather.2.cloned.1.call-start = ((), (), s32[]{:S(2)}) async-start(), calls=%async_computation.2 | async-start | bytes 21233664 | tf_op jit(solution)/shard_map/all_gather | solution.py:73
  86.9 5.4 copy-start.5
  92.3 8.0 copy-start.2
  100.3 11.5 %copy-start.6 = (f32[512,3456]{1,0:T(8,128)}, f32[512,3456]{1,0:T(8,128)S(1)}, u32[]{:S(2)}) copy-start(f32[512,3456]{1,0:T(8,128)S(1)} %fusion.19) | copy-start | bytes 21233668
  111.8 1.8 copy-start.4
  834.6 2.1 copy-start.3
Sparse Core Ops, SparseCore 0:
  115.3 360.5 all-gather.1
